TPU v7x, 32 devices: a whole 2x2x4 slice. The times are simulated.
32 devices in a mesh: area: 8 (over z, x), row: 4 (over y, core).
Axes of the slice: x: 2, y: 2, z: 4, core: 2. Of those that a mesh axis runs over, the one named last changes fastest.
Arguments:
- conductance_inverse: float32 [32, 1024, 1024], P(('area', 'row')), as said below
- cap_history: float32 [32, 1024, 128], P(('area', 'row')), may hold values from -3 to 3
- cap_conductance: float32 [32, 1024], P(('area', 'row')), may hold values from 0.5 to 0.8
- wave_history: float32 [32, 40, 32, 128], P(('area', 'row')), may hold values from -6 to 6
- line_partner: int32 [32, 32], P(('area', 'row')), may hold values from 0 to 31, as said below
- line_node: int32 [32, 32], P(('area', 'row')), may hold values from 0 to 1023
- line_delay: int32 [32, 32], P(('area', 'row')), may hold values from 20 to 40
- line_admittance: float32 [32, 32], P(('area', 'row')), may hold values from 0.2 to 1
- conv_node: int32 [32, 64], P(('area', 'row')), may hold values from 0 to 1023
- conv_count: int32 [32], P(('area', 'row')), may hold values from 1 to 64, as said below
- conv_state: float32 [32, 2, 64, 128], P(('area', 'row')), may hold values from -3 to 3
- conv_reference: float32 [32, 2, 64, 128], P(('area', 'row')), may hold values from -4 to 4
- conv_rate: float32 [32, 64], P(('area', 'row')), may hold values from 0.03 to 0.6
- conv_limit: float32 [32, 64], P(('area', 'row')), may hold values from 1 to 2.5
- port_node: int32 [32, 8], P(('area', 'row')), may hold values from 0 to 1023
- port_admittance: float32 [32, 8], P(('area', 'row')), may hold values from 0.3 to 1.2
- port_voltage_prev: float32 [2, 32, 8, 128], P(None, ('area', 'row')), may hold values from -5 to 5
- port_bus: int32 [32, 8], P('area'), may hold values from 0 to 20479
- transfer_impedance: float32 [2, 20480, 256], P(None, 'row', 'area'), may hold values from -0.75 to 0.75
Outputs:
- waves: float32 [32, 20, 32, 128], P(('area', 'row'))
- cap_history_out: float32 [32, 1024, 128], P(('area', 'row'))
- conv_state_out: float32 [32, 2, 64, 128], P(('area', 'row'))
- bus_voltage: float32 [2, 20480, 128], P(None, 'row')
- port_voltage: float32 [2, 32, 8, 128], P(None, ('area', 'row'))
Inputs may be any that keep to these rules, and one draw needn't show every extreme that they name: Slot l < 16 of subnetwork s and slot l + 16 of subnetwork (s + k_l) mod 32 are the two ends of one line, with k_l in 1 or 2 the same for every subnetwork and exactly 12 of the k_l equal to 1; so line_partner[s, l] = (s + k_l) mod 32 and line_partner[s, l + 16] = (s - k_l) mod 32. `conv_count`: some subnetwork has all 64 converters in service. `conductance_inverse`: each subnetwork's inverse nodal conductance matrix.
All inputs are finite; a program needn't handle non-finite values.
Results may differ from a plain program's by a relative error of at most 0.0003.
Values sent between devices are 32-bit elements; how exact they have to be, the bound alone decides.
A program may use at most 64 MiB of HBM per device.

v0:
```python
import math
import jax
import jax.numpy as jnp
from jax import lax
from jax.sharding import PartitionSpec as P

STEPS = 20
HIST = 40
NEAR = 12
HIGHEST = lax.Precision.HIGHEST
SAG_FACTOR = 0.3


def from_behind(x, axis, by):
    size = lax.axis_size(axis)
    return lax.ppermute(x, axis, [(i, (i + by) % size) for i in range(size)])


def window(
    ginv,
    start_hist,
    gcap,
    incoming,
    lnode,
    ladm,
    cnode,
    ccount,
    cstate,
    setpoint_flow,
    crate,
    climit,
    pnode,
    padm,
    pvolt,
):
    nodes = ginv.shape[0]
    lines = lnode.shape[0]
    convs = cnode.shape[0]
    index = jnp.concatenate([lnode, cnode, pnode])
    onehot = (jnp.arange(nodes, dtype=jnp.int32)[:, None] == index[None, :]).astype(jnp.float32)
    picker = onehot.T
    live = (jnp.arange(convs, dtype=jnp.int32) < ccount)[:, None]
    angles = jnp.arange(1, STEPS + 1, dtype=jnp.float32) * jnp.float32(2.0 * math.pi / STEPS)
    limit = climit[:, None]
    slew_limit = crate[:, None]

    def advance(carry, inputs):
        hist_now, inverter_axial_part, inverter_normal_part, acc_re, acc_im = carry
        inward, angle = inputs
        angle_cos_factor = jnp.cos(angle)
        angle_sin_factor = jnp.sin(angle)
        drive = jnp.where(
            live,
            inverter_axial_part * angle_cos_factor - inverter_normal_part * angle_sin_factor,
            0.0,
        )
        source = padm[:, None] * (pvolt[0] * angle_cos_factor - pvolt[1] * angle_sin_factor)
        stacked = jnp.concatenate([inward, drive, source], axis=0)
        right = hist_now + jnp.dot(onehot, stacked, precision=HIGHEST)
        volt = jnp.dot(ginv, right, precision=HIGHEST)
        probe = jnp.dot(picker, volt, precision=HIGHEST)
        at_line = probe[:lines]
        inverter_emf = probe[lines : lines + convs]
        at_port = probe[lines + convs :]
        outward = 2.0 * ladm[:, None] * at_line - inward
        flow = source - padm[:, None] * at_port
        acc_re = acc_re + flow * angle_cos_factor
        acc_im = acc_im - flow * angle_sin_factor
        unclipped_axial_part = (
            inverter_axial_part
            + slew_limit * (setpoint_flow[0] - inverter_axial_part)
            - SAG_FACTOR * inverter_emf * angle_cos_factor
        )
        unclipped_normal_part = (
            inverter_normal_part
            + slew_limit * (setpoint_flow[1] - inverter_normal_part)
            + SAG_FACTOR * inverter_emf * angle_sin_factor
        )
        inverter_axial_part = jnp.where(
            live, limit * jnp.tanh(unclipped_axial_part / limit), inverter_axial_part
        )
        inverter_normal_part = jnp.where(
            live, limit * jnp.tanh(unclipped_normal_part / limit), inverter_normal_part
        )
        hist_now = 2.0 * gcap[:, None] * volt - hist_now
        return ((hist_now, inverter_axial_part, inverter_normal_part, acc_re, acc_im), outward)

    zeros = jnp.zeros(pvolt.shape[1:], dtype=jnp.float32)
    carry = (start_hist, cstate[0], cstate[1], zeros, zeros)
    carry, outward = lax.scan(advance, carry, (incoming, angles))
    hist_end, inverter_axial_part, inverter_normal_part, acc_re, acc_im = carry
    current = jnp.stack([acc_re, acc_im]) * jnp.float32(2.0 / STEPS)
    return (outward, hist_end, jnp.stack([inverter_axial_part, inverter_normal_part]), current)


def per_device(
    conductance_inverse,
    cap_history,
    cap_conductance,
    wave_history,
    line_partner,
    line_node,
    line_delay,
    line_admittance,
    conv_node,
    conv_count,
    conv_state,
    conv_reference,
    conv_rate,
    conv_limit,
    port_node,
    port_admittance,
    port_voltage_prev,
    port_bus,
    transfer_impedance,
):
    subnets = lax.axis_size(("area", "row"))
    own = lax.axis_index(("area", "row"))
    history = wave_history[0]
    lines = history.shape[1]
    partner = line_partner[0]
    offset = (partner - own) % subnets
    signed = jnp.where(offset > subnets // 2, offset - subnets, offset)
    remote = (jnp.arange(lines, dtype=jnp.int32) + lines // 2) % lines
    combined = jnp.zeros(history.shape, jnp.float32)
    for reach in (1, -1, 2, -2):
        count = NEAR if abs(reach) == 1 else lines // 2 - NEAR
        sending = signed == reach
        order = jnp.argsort(jnp.where(sending, 0, 1), stable=True)[:count]
        packed = jnp.take(history, order, axis=1)
        arrived = from_behind(packed, ("area", "row"), reach)
        rank = jnp.cumsum(sending.astype(jnp.int32)) - 1
        slot = jnp.clip(rank[remote], 0, count - 1)
        picked = jnp.take(arrived, slot, axis=1)
        combined = combined + jnp.where((signed == -reach)[None, :, None], picked, 0.0)
    delay = line_delay[0]
    where_now = jnp.arange(STEPS, dtype=jnp.int32)[:, None] - delay[None, :] + HIST
    select = (where_now[:, None, :] == jnp.arange(HIST, dtype=jnp.int32)[None, :, None]).astype(
        jnp.float32
    )
    incoming = jnp.einsum("thl,hlc->tlc", select, combined, precision=HIGHEST)
    outward, hist_end, conv_out, current = window(
        conductance_inverse[0],
        cap_history[0],
        cap_conductance[0],
        incoming,
        line_node[0],
        line_admittance[0],
        conv_node[0],
        conv_count[0],
        conv_state[0],
        conv_reference[0],
        conv_rate[0],
        conv_limit[0],
        port_node[0],
        port_admittance[0],
        port_voltage_prev[:, 0],
    )
    bus_rows = transfer_impedance.shape[1]
    cases = current.shape[2]
    piece = lax.all_gather(current[:, None], "row", axis=1, tiled=True)
    members = piece.shape[1]
    ports = piece.shape[2]
    flat = piece.reshape(2, members * ports, cases)
    real = jnp.dot(transfer_impedance[0], flat[0], precision=HIGHEST) - jnp.dot(
        transfer_impedance[1], flat[1], precision=HIGHEST
    )
    imag = jnp.dot(transfer_impedance[0], flat[1], precision=HIGHEST) + jnp.dot(
        transfer_impedance[1], flat[0], precision=HIGHEST
    )
    partial_bus = jnp.stack([real, imag])
    bus_voltage = lax.psum(partial_bus, "area")
    first_row = lax.axis_index("row") * bus_rows
    local_bus = (port_bus - first_row).reshape(-1)
    pick_rows = (local_bus[:, None] == jnp.arange(bus_rows, dtype=jnp.int32)[None, :]).astype(
        jnp.float32
    )
    gathered = jnp.einsum("jb,xbc->xjc", pick_rows, bus_voltage, precision=HIGHEST)
    gathered = gathered.reshape(2, port_bus.shape[0], port_bus.shape[1], cases)
    port_voltage = lax.psum_scatter(gathered, "row", scatter_dimension=1, tiled=True)
    return (outward[None], hist_end[None], conv_out[None], bus_voltage, port_voltage)


def solution(mesh):
    placed = (
        P(("area", "row"), None, None),
        P(("area", "row"), None, None),
        P(("area", "row"), None),
        P(("area", "row"), None, None, None),
        P(("area", "row"), None),
        P(("area", "row"), None),
        P(("area", "row"), None),
        P(("area", "row"), None),
        P(("area", "row"), None),
        P(("area", "row")),
        P(("area", "row"), None, None, None),
        P(("area", "row"), None, None, None),
        P(("area", "row"), None),
        P(("area", "row"), None),
        P(("area", "row"), None),
        P(("area", "row"), None),
        P(None, ("area", "row"), None, None),
        P("area", None),
        P(None, "row", "area"),
    )
    return jax.shard_map(
        per_device,
        mesh=mesh,
        in_specs=placed,
        out_specs=(
            P(("area", "row"), None, None, None),
            P(("area", "row"), None, None),
            P(("area", "row"), None, None, None),
            P(None, "row", None),
            P(None, ("area", "row"), None, None),
        ),
        check_vma=False,
    )
```

profile of v0, /device:TPU:0, one launch (start us, length us, event | category | flops | bytes accessed | tf_op | source)
XLA Modules:
  0.0 522.5 jit_solution(1617881758800676381)
XLA Ops:
  7.9 1.6 sort.61
  9.6 1.5 copy.56
  11.7 3.0 collective-permute-start.2
  14.7 1.6 sort.62
  17.0 4.0 collective-permute-start.3
  20.9 1.6 sort.60
  23.3 0.9 collective-permute-start.1
  24.2 1.6 sort.59
  32.1 3.7 collective-permute-done
  36.5 1.4 gather_fusion.7
  37.9 2.7 convolution_bitcast_fusion.2
  40.6 254.0 %while.23 = (s32[]{:T(128)}, f32[1024,128]{0,1:T(8,128)S(1)}, f32[64,128]{1,0:T(8,128)S(1)}, f32[64,128]{1,0:T(8,128)S(1)}, f32[8,128]{1,0:T(8,128)S(1)}, /*inde...) while((s32[]{:T(128)}, f32[1024,128]{0,1:T(8,128)S(1)}, ...), condition=%wide.region_9.14_spmd.clone.clone.clone, body=%wide.region_8.13_spmd.clone.clone.clone.sunk | while | flops 1938803712 | bytes 8437999 | solution.py:90
  43.4 0.9 constant_dynamic-slice_fusion.3
  45.1 6.7 %bitcast_subtract_fusion.4 = (f32[1024,128]{0,1:T(8,128)S(1)}, f32[128,1024]{1,0:T(8,128)S(1)}) fusion(f32[1024,128]{0,1:T(8,128)S(1)} %get-tuple-element.591, f32[1024]{0:T(1024)S(1)} %bitcast.217, f32[1024,128]{0,1:T(8,128)S(1)} %fusion.99, f32[1024,1024]{1,0:T(8,128)} %get-tuple-element.624), kind=kOutput, calls=%fused_computation.18.clone.1 | convolution fusion | flops 1610874880 | bytes 6295552 | tf_op jit(solution)/shard_map/while/body/eval_jaxpr/dot_general | solution.py:60
  56.1 0.9 constant_dynamic-slice_fusion.3
  57.8 6.7 %bitcast_subtract_fusion.4 = (f32[1024,128]{0,1:T(8,128)S(1)}, f32[128,1024]{1,0:T(8,128)S(1)}) fusion(f32[1024,128]{0,1:T(8,128)S(1)} %get-tuple-element.591, f32[1024]{0:T(1024)S(1)} %bitcast.217, f32[1024,128]{0,1:T(8,128)S(1)} %fusion.99, f32[1024,1024]{1,0:T(8,128)} %get-tuple-element.624), kind=kOutput, calls=%fused_computation.18.clone.1 | convolution fusion | flops 1610874880 | bytes 6295552 | tf_op jit(solution)/shard_map/while/body/eval_jaxpr/dot_general | solution.py:60
  68.8 0.9 constant_dynamic-slice_fusion.3
  70.5 6.7 %bitcast_subtract_fusion.4 = (f32[1024,128]{0,1:T(8,128)S(1)}, f32[128,1024]{1,0:T(8,128)S(1)}) fusion(f32[1024,128]{0,1:T(8,128)S(1)} %get-tuple-element.591, f32[1024]{0:T(1024)S(1)} %bitcast.217, f32[1024,128]{0,1:T(8,128)S(1)} %fusion.99, f32[1024,1024]{1,0:T(8,128)} %get-tuple-element.624), kind=kOutput, calls=%fused_computation.18.clone.1 | convolution fusion | flops 1610874880 | bytes 6295552 | tf_op jit(solution)/shard_map/while/body/eval_jaxpr/dot_general | solution.py:60
  83.2 6.7 %bitcast_subtract_fusion.4 = (f32[1024,128]{0,1:T(8,128)S(1)}, f32[128,1024]{1,0:T(8,128)S(1)}) fusion(f32[1024,128]{0,1:T(8,128)S(1)} %get-tuple-element.591, f32[1024]{0:T(1024)S(1)} %bitcast.217, f32[1024,128]{0,1:T(8,128)S(1)} %fusion.99, f32[1024,1024]{1,0:T(8,128)} %get-tuple-element.624), kind=kOutput, calls=%fused_computation.18.clone.1 | convolution fusion | flops 1610874880 | bytes 6295552 | tf_op jit(solution)/shard_map/while/body/eval_jaxpr/dot_general | solution.py:60
  94.2 0.9 constant_dynamic-slice_fusion.3
  95.9 6.7 %bitcast_subtract_fusion.4 = (f32[1024,128]{0,1:T(8,128)S(1)}, f32[128,1024]{1,0:T(8,128)S(1)}) fusion(f32[1024,128]{0,1:T(8,128)S(1)} %get-tuple-element.591, f32[1024]{0:T(1024)S(1)} %bitcast.217, f32[1024,128]{0,1:T(8,128)S(1)} %fusion.99, f32[1024,1024]{1,0:T(8,128)} %get-tuple-element.624), kind=kOutput, calls=%fused_computation.18.clone.1 | convolution fusion | flops 1610874880 | bytes 6295552 | tf_op jit(solution)/shard_map/while/body/eval_jaxpr/dot_general | solution.py:60
  108.6 6.7 %bitcast_subtract_fusion.4 = (f32[1024,128]{0,1:T(8,128)S(1)}, f32[128,1024]{1,0:T(8,128)S(1)}) fusion(f32[1024,128]{0,1:T(8,128)S(1)} %get-tuple-element.591, f32[1024]{0:T(1024)S(1)} %bitcast.217, f32[1024,128]{0,1:T(8,128)S(1)} %fusion.99, f32[1024,1024]{1,0:T(8,128)} %get-tuple-element.624), kind=kOutput, calls=%fused_computation.18.clone.1 | convolution fusion | flops 1610874880 | bytes 6295552 | tf_op jit(solution)/shard_map/while/body/eval_jaxpr/dot_general | solution.py:60
  121.3 6.7 %bitcast_subtract_fusion.4 = (f32[1024,128]{0,1:T(8,128)S(1)}, f32[128,1024]{1,0:T(8,128)S(1)}) fusion(f32[1024,128]{0,1:T(8,128)S(1)} %get-tuple-element.591, f32[1024]{0:T(1024)S(1)} %bitcast.217, f32[1024,128]{0,1:T(8,128)S(1)} %fusion.99, f32[1024,1024]{1,0:T(8,128)} %get-tuple-element.624), kind=kOutput, calls=%fused_computation.18.clone.1 | convolution fusion | flops 1610874880 | bytes 6295552 | tf_op jit(solution)/shard_map/while/body/eval_jaxpr/dot_general | solution.py:60
  134.0 6.7 %bitcast_subtract_fusion.4 = (f32[1024,128]{0,1:T(8,128)S(1)}, f32[128,1024]{1,0:T(8,128)S(1)}) fusion(f32[1024,128]{0,1:T(8,128)S(1)} %get-tuple-element.591, f32[1024]{0:T(1024)S(1)} %bitcast.217, f32[1024,128]{0,1:T(8,128)S(1)} %fusion.99, f32[1024,1024]{1,0:T(8,128)} %get-tuple-element.624), kind=kOutput, calls=%fused_computation.18.clone.1 | convolution fusion | flops 1610874880 | bytes 6295552 | tf_op jit(solution)/shard_map/while/body/eval_jaxpr/dot_general | solution.py:60
  146.7 6.7 %bitcast_subtract_fusion.4 = (f32[1024,128]{0,1:T(8,128)S(1)}, f32[128,1024]{1,0:T(8,128)S(1)}) fusion(f32[1024,128]{0,1:T(8,128)S(1)} %get-tuple-element.591, f32[1024]{0:T(1024)S(1)} %bitcast.217, f32[1024,128]{0,1:T(8,128)S(1)} %fusion.99, f32[1024,1024]{1,0:T(8,128)} %get-tuple-element.624), kind=kOutput, calls=%fused_computation.18.clone.1 | convolution fusion | flops 1610874880 | bytes 6295552 | tf_op jit(solution)/shard_map/while/body/eval_jaxpr/dot_general | solution.py:60
  159.4 6.7 %bitcast_subtract_fusion.4 = (f32[1024,128]{0,1:T(8,128)S(1)}, f32[128,1024]{1,0:T(8,128)S(1)}) fusion(f32[1024,128]{0,1:T(8,128)S(1)} %get-tuple-element.591, f32[1024]{0:T(1024)S(1)} %bitcast.217, f32[1024,128]{0,1:T(8,128)S(1)} %fusion.99, f32[1024,1024]{1,0:T(8,128)} %get-tuple-element.624), kind=kOutput, calls=%fused_computation.18.clone.1 | convolution fusion | flops 1610874880 | bytes 6295552 | tf_op jit(solution)/shard_map/while/body/eval_jaxpr/dot_general | solution.py:60
  172.1 6.7 %bitcast_subtract_fusion.4 = (f32[1024,128]{0,1:T(8,128)S(1)}, f32[128,1024]{1,0:T(8,128)S(1)}) fusion(f32[1024,128]{0,1:T(8,128)S(1)} %get-tuple-element.591, f32[1024]{0:T(1024)S(1)} %bitcast.217, f32[1024,128]{0,1:T(8,128)S(1)} %fusion.99, f32[1024,1024]{1,0:T(8,128)} %get-tuple-element.624), kind=kOutput, calls=%fused_computation.18.clone.1 | convolution fusion | flops 1610874880 | bytes 6295552 | tf_op jit(solution)/shard_map/while/body/eval_jaxpr/dot_general | solution.py:60
  184.8 6.7 %bitcast_subtract_fusion.4 = (f32[1024,128]{0,1:T(8,128)S(1)}, f32[128,1024]{1,0:T(8,128)S(1)}) fusion(f32[1024,128]{0,1:T(8,128)S(1)} %get-tuple-element.591, f32[1024]{0:T(1024)S(1)} %bitcast.217, f32[1024,128]{0,1:T(8,128)S(1)} %fusion.99, f32[1024,1024]{1,0:T(8,128)} %get-tuple-element.624), kind=kOutput, calls=%fused_computation.18.clone.1 | convolution fusion | flops 1610874880 | bytes 6295552 | tf_op jit(solution)/shard_map/while/body/eval_jaxpr/dot_general | solution.py:60
  197.5 6.7 %bitcast_subtract_fusion.4 = (f32[1024,128]{0,1:T(8,128)S(1)}, f32[128,1024]{1,0:T(8,128)S(1)}) fusion(f32[1024,128]{0,1:T(8,128)S(1)} %get-tuple-element.591, f32[1024]{0:T(1024)S(1)} %bitcast.217, f32[1024,128]{0,1:T(8,128)S(1)} %fusion.99, f32[1024,1024]{1,0:T(8,128)} %get-tuple-element.624), kind=kOutput, calls=%fused_computation.18.clone.1 | convolution fusion | flops 1610874880 | bytes 6295552 | tf_op jit(solution)/shard_map/while/body/eval_jaxpr/dot_general | solution.py:60
  210.2 6.7 %bitcast_subtract_fusion.4 = (f32[1024,128]{0,1:T(8,128)S(1)}, f32[128,1024]{1,0:T(8,128)S(1)}) fusion(f32[1024,128]{0,1:T(8,128)S(1)} %get-tuple-element.591, f32[1024]{0:T(1024)S(1)} %bitcast.217, f32[1024,128]{0,1:T(8,128)S(1)} %fusion.99, f32[1024,1024]{1,0:T(8,128)} %get-tuple-element.624), kind=kOutput, calls=%fused_computation.18.clone.1 | convolution fusion | flops 1610874880 | bytes 6295552 | tf_op jit(solution)/shard_map/while/body/eval_jaxpr/dot_general | solution.py:60
  222.9 6.7 %bitcast_subtract_fusion.4 = (f32[1024,128]{0,1:T(8,128)S(1)}, f32[128,1024]{1,0:T(8,128)S(1)}) fusion(f32[1024,128]{0,1:T(8,128)S(1)} %get-tuple-element.591, f32[1024]{0:T(1024)S(1)} %bitcast.217, f32[1024,128]{0,1:T(8,128)S(1)} %fusion.99, f32[1024,1024]{1,0:T(8,128)} %get-tuple-element.624), kind=kOutput, calls=%fused_computation.18.clone.1 | convolution fusion | flops 1610874880 | bytes 6295552 | tf_op jit(solution)/shard_map/while/body/eval_jaxpr/dot_general | solution.py:60
  235.6 6.7 %bitcast_subtract_fusion.4 = (f32[1024,128]{0,1:T(8,128)S(1)}, f32[128,1024]{1,0:T(8,128)S(1)}) fusion(f32[1024,128]{0,1:T(8,128)S(1)} %get-tuple-element.591, f32[1024]{0:T(1024)S(1)} %bitcast.217, f32[1024,128]{0,1:T(8,128)S(1)} %fusion.99, f32[1024,1024]{1,0:T(8,128)} %get-tuple-element.624), kind=kOutput, calls=%fused_computation.18.clone.1 | convolution fusion | flops 1610874880 | bytes 6295552 | tf_op jit(solution)/shard_map/while/body/eval_jaxpr/dot_general | solution.py:60
  248.3 6.7 %bitcast_subtract_fusion.4 = (f32[1024,128]{0,1:T(8,128)S(1)}, f32[128,1024]{1,0:T(8,128)S(1)}) fusion(f32[1024,128]{0,1:T(8,128)S(1)} %get-tuple-element.591, f32[1024]{0:T(1024)S(1)} %bitcast.217, f32[1024,128]{0,1:T(8,128)S(1)} %fusion.99, f32[1024,1024]{1,0:T(8,128)} %get-tuple-element.624), kind=kOutput, calls=%fused_computation.18.clone.1 | convolution fusion | flops 1610874880 | bytes 6295552 | tf_op jit(solution)/shard_map/while/body/eval_jaxpr/dot_general | solution.py:60
  261.0 6.7 %bitcast_subtract_fusion.4 = (f32[1024,128]{0,1:T(8,128)S(1)}, f32[128,1024]{1,0:T(8,128)S(1)}) fusion(f32[1024,128]{0,1:T(8,128)S(1)} %get-tuple-element.591, f32[1024]{0:T(1024)S(1)} %bitcast.217, f32[1024,128]{0,1:T(8,128)S(1)} %fusion.99, f32[1024,1024]{1,0:T(8,128)} %get-tuple-element.624), kind=kOutput, calls=%fused_computation.18.clone.1 | convolution fusion | flops 1610874880 | bytes 6295552 | tf_op jit(solution)/shard_map/while/body/eval_jaxpr/dot_general | solution.py:60
  273.7 6.7 %bitcast_subtract_fusion.4 = (f32[1024,128]{0,1:T(8,128)S(1)}, f32[128,1024]{1,0:T(8,128)S(1)}) fusion(f32[1024,128]{0,1:T(8,128)S(1)} %get-tuple-element.591, f32[1024]{0:T(1024)S(1)} %bitcast.217, f32[1024,128]{0,1:T(8,128)S(1)} %fusion.99, f32[1024,1024]{1,0:T(8,128)} %get-tuple-element.624), kind=kOutput, calls=%fused_computation.18.clone.1 | convolution fusion | flops 1610874880 | bytes 6295552 | tf_op jit(solution)/shard_map/while/body/eval_jaxpr/dot_general | solution.py:60
  286.4 6.7 %bitcast_subtract_fusion.4 = (f32[1024,128]{0,1:T(8,128)S(1)}, f32[128,1024]{1,0:T(8,128)S(1)}) fusion(f32[1024,128]{0,1:T(8,128)S(1)} %get-tuple-element.591, f32[1024]{0:T(1024)S(1)} %bitcast.217, f32[1024,128]{0,1:T(8,128)S(1)} %fusion.99, f32[1024,1024]{1,0:T(8,128)} %get-tuple-element.624), kind=kOutput, calls=%fused_computation.18.clone.1 | convolution fusion | flops 1610874880 | bytes 6295552 | tf_op jit(solution)/shard_map/while/body/eval_jaxpr/dot_general | solution.py:60
  294.6 5.4 %all_gather.3 = f32[2,4,8,128]{3,2,1,0:T(8,128)S(1)} all-gather(f32[2,1,8,128]{3,2,1,0:T(8,128)S(1)} %maximum_multiply_fusion), channel_id=1, replica_groups=mesh['area'=8,'row'=4] {'row'}, dimensions={1}, use_global_device_ids=true | all-gather | bytes 40960 | tf_op jit(solution)/shard_map/all_gather | solution.py:161
  300.0 2.2 fusion.39
  302.2 2.2 fusion.41
  304.5 2.3 fusion.36
  306.8 2.3 fusion.35
  309.0 2.9 pad_maximum_fusion
  313.4 1.0 copy.48
  315.0 177.5 %all-reduce.3.cloned.1.call-done = f32[2,5120,128]{1,2,0:T(8,128)} async-done(((f32[2,5120,128]{1,2,0:T(8,128)}), f32[2,5120,128]{1,2,0:T(8,128)}) %all-reduce.3.cloned.1.call-update) | async-done | bytes 5242896 | tf_op jit(solution)/shard_map/psum | solution.py:172
  492.5 5.2 convolution_bitcast_fusion.3
  497.7 10.9 %all-reduce = f32[2,4,8,128]{3,2,1,0:T(8,128)S(1)} all-reduce(f32[2,4,8,128]{3,2,1,0:T(8,128)S(1)} %convolution_bitcast_fusion.3), channel_id=2, replica_groups=mesh['area'=8,'row'=4] {'row'}, use_global_device_ids=true, to_apply=%region_11.16.clone | all-reduce | flops 8192 | bytes 65536
  508.6 1.2 constant_dynamic-slice_fusion.1
  509.8 5.9 %copy.50 = f32[2,5120,128]{2,1,0:T(8,128)} copy(f32[2,5120,128]{1,2,0:T(8,128)} %all-reduce.3.cloned.1.call-done) | data formatting | bytes 10485760
  (338 shorter events, 97.4 us)
Async XLA Ops:
  7.2 19.4 %copy-start.11 = (s32[1,32]{1,0:T(1,128)S(1)}, s32[1,32]{1,0:T(1,128)}, u32[]{:S(2)}) copy-start(s32[1,32]{1,0:T(1,128)} %param.33) | copy-start | bytes 388
  7.2 19.6 %copy-start.10 = (s32[1,32]{1,0:T(1,128)S(1)}, s32[1,32]{1,0:T(1,128)}, u32[]{:S(2)}) copy-start(s32[1,32]{1,0:T(1,128)} %param.35) | copy-start | bytes 388
  7.2 485.3 %all-reduce.3.cloned.1.call-start = ((), (), s32[]{:S(2)}) async-start(), calls=%async_computation | async-start | bytes 10485760 | tf_op jit(solution)/shard_map/psum | solution.py:172
  11.6 18.9 %copy-start.5 = (f32[1,2,64,128]{3,2,1,0:T(8,128)S(1)}, f32[1,2,64,128]{3,2,1,0:T(8,128)}, u32[]{:S(2)}) copy-start(f32[1,2,64,128]{3,2,1,0:T(8,128)} %param.39) | copy-start | bytes 196612
  11.7 19.8 %collective-permute-start.2 = (f32[40,4,128]{2,0,1:T(8,128)S(1)}, f32[40,4,128]{2,0,1:T(8,128)S(1)}, u32[]{:S(2)}, u32[]{:S(2)}) collective-permute-start(f32[40,4,128]{2,0,1:T(8,128)S(1)} %select_bitcast_fusion.3), channel_id=1, source_target_pairs={{0,2},{1,3},{2,4},{3,5},{4,6},{5,7},{6,8},{7,9},{8,10},{9,11},{10,... | collective-permute-start | bytes 245768 | tf_op jit(solution)/shard_map/ppermute | solution.py:16
  16.3 14.3 %copy-start.3 = (f32[1,1024,128]{2,1,0:T(8,128)S(1)}, f32[1,1024,128]{2,1,0:T(8,128)}, u32[]{:S(2)}) copy-start(f32[1,1024,128]{2,1,0:T(8,128)} %param.30) | copy-start | bytes 1572868
  17.0 13.9 %collective-permute-start.3 = (f32[40,4,128]{2,0,1:T(8,128)S(1)}, f32[40,4,128]{2,0,1:T(8,128)S(1)}, u32[]{:S(2)}, u32[]{:S(2)}) collective-permute-start(f32[40,4,128]{2,0,1:T(8,128)S(1)} %select_bitcast_fusion.2), channel_id=1, source_target_pairs={{0,30},{1,31},{2,0},{3,1},{4,2},{5,3},{6,4},{7,5},{8,6},{9,7},{10,... | collective-permute-start | bytes 245768 | tf_op jit(solution)/shard_map/ppermute | solution.py:16
  23.1 7.7 %copy-start.12 = (s32[1,8]{1,0:T(1,128)S(1)}, s32[1,8]{1,0:T(1,128)}, u32[]{:S(2)}) copy-start(s32[1,8]{1,0:T(1,128)} %param.43) | copy-start | bytes 100
  23.1 7.7 %copy-start.13 = (s32[1,64]{1,0:T(1,128)S(1)}, s32[1,64]{1,0:T(1,128)}, u32[]{:S(2)}) copy-start(s32[1,64]{1,0:T(1,128)} %param.37) | copy-start | bytes 772
  23.2 7.6 %copy-start.14 = (s32[1,32]{1,0:T(1,128)S(1)}, s32[1,32]{1,0:T(1,128)}, u32[]{:S(2)}) copy-start(s32[1,32]{1,0:T(1,128)} %param.34) | copy-start | bytes 388
  23.3 13.2 %collective-permute-start.1 = (f32[40,12,128]{2,0,1:T(8,128)S(1)}, f32[40,12,128]{2,0,1:T(8,128)S(1)}, u32[]{:S(2)}, u32[]{:S(2)}) collective-permute-start(f32[40,12,128]{2,0,1:T(8,128)S(1)} %select_bitcast_fusion), channel_id=1, source_target_pairs={{0,31},{1,0},{2,1},{3,2},{4,3},{5,4},{6,5},{7,6},{8,7},{9,8},{10,9... | collective-permute-start | bytes 737288 | tf_op jit(solution)/shard_map/ppermute | solution.py:16
  26.5 9.3 %collective-permute-start = (f32[40,12,128]{2,0,1:T(8,128)S(1)}, f32[40,12,128]{2,0,1:T(8,128)S(1)}, u32[]{:S(2)}, u32[]{:S(2)}) collective-permute-start(f32[40,12,128]{2,0,1:T(8,128)S(1)} %select_bitcast_fusion.1), channel_id=1, source_target_pairs={{0,1},{1,2},{2,3},{3,4},{4,5},{5,6},{6,7},{7,8},{8,9},{9,10},{10,1... | collective-permute-start | bytes 737288 | tf_op jit(solution)/shard_map/ppermute | solution.py:16
  36.4 4.2 copy-start.1
  36.4 4.2 copy-start.2
  36.4 4.2 copy-start.4
  36.4 4.2 copy-start.6
  36.4 4.2 copy-start.7
  36.4 4.2 copy-start.8
  36.4 4.2 copy-start.15
  40.6 259.4 %copy-start = (f32[2,5120,32]{1,2,0:T(8,128)S(1)}, f32[2,5120,32]{1,2,0:T(8,128)}, u32[]{:S(2)}) copy-start(f32[2,5120,32]{1,2,0:T(8,128)} %param.47) | copy-start | bytes 3932164
  312.0 0.7 copy-start.9
  312.0 0.8 copy-start.16
Sparse Core Ops, SparseCore 0:
  312.1 180.2 all-reduce.2
where the time goes:
time: 525 us; the launch traced here: 523 us
  waiting for transfers between devices  181 us (34%)
  matrix products  178 us (34%)
  local copies, waits for them, and re-layouts  49.6 us (9%)
  other arithmetic  45.4 us (9%)
  loops' own time  29.9 us (6%)
  blocking collectives  16.3 us (3%)
  between operations  14.6 us (3%)
  starting transfers between devices  8.01 us (2%)
    psum x1, waiting for transfers between devices, per_device(): bus_voltage = lax.psum(partial_bus, 'area')  177 us
    dot_general x20, matrix products, advance(): volt = jnp.dot(ginv, right, precision=HIGHEST)  134 us
    dynamic_slice x40, local copies, waits for them, and re-layouts, window(): carry, outward = lax.scan(advance, carry, (incoming, angles))  30 us
    another operation x1, loops' own time, window(): carry, outward = lax.scan(advance, carry, (incoming, angles))  29.9 us
    dynamic_update_slice x20, other arithmetic, window(): carry, outward = lax.scan(advance, carry, (incoming, angles))  13.7 us
    dot_general x20, matrix products, advance(): probe = jnp.dot(picker, volt, precision=HIGHEST)  13.4 us
    broadcast_in_dim x20, other arithmetic, advance(): jnp.where(live, inverter_axial_part * angle_cos_factor - inverter_normal_...  13.1 us
    dot_general x20, matrix products, advance(): right = hist_now + jnp.dot(onehot, stacked, precision=HIGHEST)  12.9 us
  transfers between devices with their start and end apart: 5, of which 2 were waited for; matrix products, arithmetic and copies ran while one was open for 3% of the time, Pallas kernels for 0%

commit v1 on v0

--- a/solution.py
+++ b/solution.py
@@ -169,7 +169,11 @@
         transfer_impedance[1], flat[0], precision=HIGHEST
     )
     partial_bus = jnp.stack([real, imag])
-    bus_voltage = lax.psum(partial_bus, "area")
+    bus_voltage = partial_bus
+    for hop in (1, 2, 4):
+        bus_voltage = bus_voltage + lax.ppermute(
+            bus_voltage, "area", [(dev, dev ^ hop) for dev in range(8)]
+        )
     first_row = lax.axis_index("row") * bus_rows
     local_bus = (port_bus - first_row).reshape(-1)
     pick_rows = (local_bus[:, None] == jnp.arange(bus_rows, dtype=jnp.int32)[None, :]).astype(

time: 525 us -> 818 us (1.56)
  waiting for transfers between devices: 181 us -> 452 us
  other arithmetic: 45.4 us -> 61.5 us
  local copies, waits for them, and re-layouts: 49.6 us -> 63.4 us
  between operations: 14.6 us -> 1.06 us
    ppermute x0 -> x3, waiting for transfers between devices: none -> 452 us  [per_device(): lax.ppermute(bus_voltage, 'area', [(dev, dev ^ hop) for dev in range(8)])]
    psum x1 -> x0, waiting for transfers between devices: 177 us -> none  [per_device(): bus_voltage = lax.psum(partial_bus, 'area')]
    add x0 -> x3, other arithmetic: none -> 14.1 us  [per_device(): bus_voltage + lax.ppermute(bus_voltage, 'area', [(dev, dev ^ hop) for dev...]
    dynamic_slice x40, local copies, waits for them, and re-layouts: 30 us -> 43.9 us  [window(): carry, outward = lax.scan(advance, carry, (incoming, angles))]
  transfers between devices with their start and end apart: 5 -> 7, of which waited for: 2 -> 3; matrix products, arithmetic and copies ran while one was open for 3% -> 2% of each run, Pallas kernels for 0% -> 0%
where the time goes in v1:
time: 818 us; the launch traced here: 816 us
  waiting for transfers between devices  452 us (55%)
  matrix products  178 us (22%)
  local copies, waits for them, and re-layouts  63.4 us (8%)
  other arithmetic  61.5 us (8%)
  loops' own time  30.3 us (4%)
  blocking collectives  15.6 us (2%)
  starting transfers between devices  13.9 us (2%)
    ppermute x3, waiting for transfers between devices, per_device(): lax.ppermute(bus_voltage, 'area', [(dev, dev ^ hop) for dev in range(8)])  452 us
    dot_general x20, matrix products, advance(): volt = jnp.dot(ginv, right, precision=HIGHEST)  134 us
    dynamic_slice x40, local copies, waits for them, and re-layouts, window(): carry, outward = lax.scan(advance, carry, (incoming, angles))  43.9 us
    another operation x1, loops' own time, window(): carry, outward = lax.scan(advance, carry, (incoming, angles))  30.3 us
  transfers between devices with their start and end apart: 7, of which 3 were waited for; matrix products, arithmetic and copies ran while one was open for 2% of the time, Pallas kernels for 0%

profile of v1, /device:TPU:0, one launch (start us, length us, event | category | flops | bytes accessed | tf_op | source)
XLA Modules:
  0.0 815.8 jit_solution(4600437952398727485)
XLA Ops:
  0.7 1.5 copy.56
  3.5 1.6 sort.62
  5.7 7.0 collective-permute-start.3
  12.7 1.6 sort.61
  15.0 1.6 sort.60
  17.3 4.5 collective-permute-start.1
  21.8 1.6 sort.59
  34.4 1.5 gather_fusion.5
  36.0 2.7 convolution_bitcast_fusion.2
  38.8 268.4 %while.23 = (s32[]{:T(128)}, f32[1024,128]{0,1:T(8,128)S(1)}, f32[64,128]{1,0:T(8,128)S(1)}, f32[64,128]{1,0:T(8,128)S(1)}, f32[8,128]{1,0:T(8,128)S(1)}, /*inde...) while((s32[]{:T(128)}, f32[1024,128]{0,1:T(8,128)S(1)}, ...), condition=%wide.region_9.14_spmd.clone.clone.clone, body=%wide.region_8.13_spmd.clone.clone.clone.sunk | while | flops 1938803712 | bytes 8439591 | solution.py:90
  38.8 1.4 dynamic_slice.18
  44.0 6.7 bitcast_subtract_fusion.4
  52.3 1.3 dynamic_slice.18
  57.4 6.7 bitcast_subtract_fusion.4
  65.7 1.3 dynamic_slice.18
  70.8 6.7 bitcast_subtract_fusion.4
  84.3 6.7 bitcast_subtract_fusion.4
  97.7 6.7 bitcast_subtract_fusion.4
  111.1 6.7 bitcast_subtract_fusion.4
  124.5 6.7 bitcast_subtract_fusion.4
  137.9 6.7 bitcast_subtract_fusion.4
  151.3 6.7 bitcast_subtract_fusion.4
  164.7 6.7 bitcast_subtract_fusion.4
  178.2 6.7 bitcast_subtract_fusion.4
  191.6 6.7 bitcast_subtract_fusion.4
  205.0 6.7 bitcast_subtract_fusion.4
  218.4 6.7 bitcast_subtract_fusion.4
  231.8 6.7 bitcast_subtract_fusion.4
  245.2 6.7 bitcast_subtract_fusion.4
  258.6 6.7 bitcast_subtract_fusion.4
  272.1 6.7 bitcast_subtract_fusion.4
  285.5 6.7 bitcast_subtract_fusion.4
  298.9 6.7 bitcast_subtract_fusion.4
  307.2 5.4 all_gather.3
  312.5 2.2 fusion.39
  314.8 2.2 fusion.41
  317.0 2.2 fusion.36
  319.3 2.2 fusion.35
  322.0 115.3 %collective-permute-done.4 = f32[2,5120,128]{1,2,0:T(8,128)S(1)} collective-permute-done((f32[2,5120,128]{1,2,0:T(8,128)S(1)}, f32[2,5120,128]{1,2,0:T(8,128)S(1)}, u32[]{:S(2)}, u32[]{:S(2)}) %collective-permute-start.4) | collective-permute-done | bytes 5242912 | tf_op jit(solution)/shard_map/ppermute | solution.py:174
  438.2 114.5 %collective-permute-done.5 = f32[2,5120,128]{1,2,0:T(8,128)} collective-permute-done((f32[2,5120,128]{1,2,0:T(8,128)S(1)}, f32[2,5120,128]{1,2,0:T(8,128)}, u32[]{:S(2)}, u32[]{:S(2)}) %collective-permute-start.5) | collective-permute-done | bytes 5242912 | tf_op jit(solution)/shard_map/ppermute | solution.py:174
  552.7 6.1 fusion.85
  558.8 2.2 collective-permute-start.6
  563.3 222.7 %collective-permute-done.6 = f32[2,5120,128]{1,2,0:T(8,128)} collective-permute-done((f32[2,5120,128]{1,2,0:T(8,128)}, f32[2,5120,128]{1,2,0:T(8,128)}, u32[]{:S(2)}, u32[]{:S(2)}) %collective-permute-start.6) | collective-permute-done | bytes 5242912 | tf_op jit(solution)/shard_map/ppermute | solution.py:174
  786.0 7.2 add.227
  793.2 5.9 copy.50
  799.1 5.2 convolution_bitcast_fusion.3
  804.3 10.3 %all-reduce = f32[2,4,8,128]{3,2,1,0:T(8,128)S(1)} all-reduce(f32[2,4,8,128]{3,2,1,0:T(8,128)S(1)} %convolution_bitcast_fusion.3), channel_id=2, replica_groups=mesh['area'=8,'row'=4] {'row'}, use_global_device_ids=true, to_apply=%region_10.15.clone | all-reduce | flops 8192 | bytes 65536
  814.6 1.3 constant_dynamic-slice_fusion.1
  (420 shorter events, 117.6 us)
Async XLA Ops:
  0.6 23.5 %copy-start.11 = (s32[1,32]{1,0:T(1,128)S(1)}, s32[1,32]{1,0:T(1,128)}, u32[]{:S(2)}) copy-start(s32[1,32]{1,0:T(1,128)} %param.33) | copy-start | bytes 388
  0.6 24.3 %copy-start.5 = (f32[1,2,64,128]{3,2,1,0:T(8,128)S(1)}, f32[1,2,64,128]{3,2,1,0:T(8,128)}, u32[]{:S(2)}) copy-start(f32[1,2,64,128]{3,2,1,0:T(8,128)} %param.39) | copy-start | bytes 196612
  0.7 29.6 %copy-start.10 = (s32[1,32]{1,0:T(1,128)S(1)}, s32[1,32]{1,0:T(1,128)}, u32[]{:S(2)}) copy-start(s32[1,32]{1,0:T(1,128)} %param.35) | copy-start | bytes 388
  0.7 30.9 %copy-start.3 = (f32[1,1024,128]{2,1,0:T(8,128)S(1)}, f32[1,1024,128]{2,1,0:T(8,128)}, u32[]{:S(2)}) copy-start(f32[1,1024,128]{2,1,0:T(8,128)} %param.30) | copy-start | bytes 1572868
  0.7 31.7 %copy-start.12 = (s32[1,8]{1,0:T(1,128)S(1)}, s32[1,8]{1,0:T(1,128)}, u32[]{:S(2)}) copy-start(s32[1,8]{1,0:T(1,128)} %param.43) | copy-start | bytes 100
  0.7 31.7 %copy-start.13 = (s32[1,64]{1,0:T(1,128)S(1)}, s32[1,64]{1,0:T(1,128)}, u32[]{:S(2)}) copy-start(s32[1,64]{1,0:T(1,128)} %param.37) | copy-start | bytes 772
  0.7 31.7 %copy-start.14 = (s32[1,32]{1,0:T(1,128)S(1)}, s32[1,32]{1,0:T(1,128)}, u32[]{:S(2)}) copy-start(s32[1,32]{1,0:T(1,128)} %param.34) | copy-start | bytes 388
  5.7 26.7 %collective-permute-start.3 = (f32[40,4,128]{2,0,1:T(8,128)S(1)}, f32[40,4,128]{2,0,1:T(8,128)S(1)}, u32[]{:S(2)}, u32[]{:S(2)}) collective-permute-start(f32[40,4,128]{2,0,1:T(8,128)S(1)} %select_bitcast_fusion.2), channel_id=1, source_target_pairs={{0,30},{1,31},{2,0},{3,1},{4,2},{5,3},{6,4},{7,5},{8,6},{9,7},{10,... | collective-permute-start | bytes 245768 | tf_op jit(solution)/shard_map/ppermute | solution.py:16
  14.9 18.1 %collective-permute-start.2 = (f32[40,4,128]{2,0,1:T(8,128)S(1)}, f32[40,4,128]{2,0,1:T(8,128)S(1)}, u32[]{:S(2)}, u32[]{:S(2)}) collective-permute-start(f32[40,4,128]{2,0,1:T(8,128)S(1)} %select_bitcast_fusion.3), channel_id=1, source_target_pairs={{0,2},{1,3},{2,4},{3,5},{4,6},{5,7},{6,8},{7,9},{8,10},{9,11},{10,... | collective-permute-start | bytes 245768 | tf_op jit(solution)/shard_map/ppermute | solution.py:16
  17.3 16.4 %collective-permute-start.1 = (f32[40,12,128]{2,0,1:T(8,128)S(1)}, f32[40,12,128]{2,0,1:T(8,128)S(1)}, u32[]{:S(2)}, u32[]{:S(2)}) collective-permute-start(f32[40,12,128]{2,0,1:T(8,128)S(1)} %select_bitcast_fusion), channel_id=1, source_target_pairs={{0,31},{1,0},{2,1},{3,2},{4,3},{5,4},{6,5},{7,6},{8,7},{9,8},{10,9... | collective-permute-start | bytes 737288 | tf_op jit(solution)/shard_map/ppermute | solution.py:16
  24.1 10.3 %collective-permute-start = (f32[40,12,128]{2,0,1:T(8,128)S(1)}, f32[40,12,128]{2,0,1:T(8,128)S(1)}, u32[]{:S(2)}, u32[]{:S(2)}) collective-permute-start(f32[40,12,128]{2,0,1:T(8,128)S(1)} %select_bitcast_fusion.1), channel_id=1, source_target_pairs={{0,1},{1,2},{2,3},{3,4},{4,5},{5,6},{6,7},{7,8},{8,9},{9,10},{10,1... | collective-permute-start | bytes 737288 | tf_op jit(solution)/shard_map/ppermute | solution.py:16
  38.7 273.8 %copy-start = (f32[2,5120,32]{1,2,0:T(8,128)S(1)}, f32[2,5120,32]{1,2,0:T(8,128)}, u32[]{:S(2)}) copy-start(f32[2,5120,32]{1,2,0:T(8,128)} %param.47) | copy-start | bytes 3932164
  38.8 12.6 %copy-start.8 = (f32[64,1]{0,1:T(1,128)S(1)}, f32[64,1]{0,1:T(1,128)}, u32[]{:S(2)}) copy-start(f32[64,1]{0,1:T(1,128)} %get-tuple-element.626) | copy-start | bytes 772 | tf_op jit(solution)/shard_map/while
  42.3 9.3 %copy-start.15 = (f32[1,32]{1,0:T(1,128)S(1)}, f32[1,32]{1,0:T(1,128)}, u32[]{:S(2)}) copy-start(f32[1,32]{1,0:T(1,128)} %get-tuple-element.628) | copy-start | bytes 388 | tf_op jit(solution)/shard_map/while
  52.3 12.5 %copy-start.8 = (f32[64,1]{0,1:T(1,128)S(1)}, f32[64,1]{0,1:T(1,128)}, u32[]{:S(2)}) copy-start(f32[64,1]{0,1:T(1,128)} %get-tuple-element.626) | copy-start | bytes 772 | tf_op jit(solution)/shard_map/while
  55.8 9.3 %copy-start.15 = (f32[1,32]{1,0:T(1,128)S(1)}, f32[1,32]{1,0:T(1,128)}, u32[]{:S(2)}) copy-start(f32[1,32]{1,0:T(1,128)} %get-tuple-element.628) | copy-start | bytes 388 | tf_op jit(solution)/shard_map/while
  65.7 12.5 %copy-start.8 = (f32[64,1]{0,1:T(1,128)S(1)}, f32[64,1]{0,1:T(1,128)}, u32[]{:S(2)}) copy-start(f32[64,1]{0,1:T(1,128)} %get-tuple-element.626) | copy-start | bytes 772 | tf_op jit(solution)/shard_map/while
  69.2 9.3 %copy-start.15 = (f32[1,32]{1,0:T(1,128)S(1)}, f32[1,32]{1,0:T(1,128)}, u32[]{:S(2)}) copy-start(f32[1,32]{1,0:T(1,128)} %get-tuple-element.628) | copy-start | bytes 388 | tf_op jit(solution)/shard_map/while
  79.1 12.5 %copy-start.8 = (f32[64,1]{0,1:T(1,128)S(1)}, f32[64,1]{0,1:T(1,128)}, u32[]{:S(2)}) copy-start(f32[64,1]{0,1:T(1,128)} %get-tuple-element.626) | copy-start | bytes 772 | tf_op jit(solution)/shard_map/while
  82.6 9.3 %copy-start.15 = (f32[1,32]{1,0:T(1,128)S(1)}, f32[1,32]{1,0:T(1,128)}, u32[]{:S(2)}) copy-start(f32[1,32]{1,0:T(1,128)} %get-tuple-element.628) | copy-start | bytes 388 | tf_op jit(solution)/shard_map/while
  92.5 12.5 %copy-start.8 = (f32[64,1]{0,1:T(1,128)S(1)}, f32[64,1]{0,1:T(1,128)}, u32[]{:S(2)}) copy-start(f32[64,1]{0,1:T(1,128)} %get-tuple-element.626) | copy-start | bytes 772 | tf_op jit(solution)/shard_map/while
  96.0 9.3 %copy-start.15 = (f32[1,32]{1,0:T(1,128)S(1)}, f32[1,32]{1,0:T(1,128)}, u32[]{:S(2)}) copy-start(f32[1,32]{1,0:T(1,128)} %get-tuple-element.628) | copy-start | bytes 388 | tf_op jit(solution)/shard_map/while
  106.0 12.5 %copy-start.8 = (f32[64,1]{0,1:T(1,128)S(1)}, f32[64,1]{0,1:T(1,128)}, u32[]{:S(2)}) copy-start(f32[64,1]{0,1:T(1,128)} %get-tuple-element.626) | copy-start | bytes 772 | tf_op jit(solution)/shard_map/while
  109.4 9.3 %copy-start.15 = (f32[1,32]{1,0:T(1,128)S(1)}, f32[1,32]{1,0:T(1,128)}, u32[]{:S(2)}) copy-start(f32[1,32]{1,0:T(1,128)} %get-tuple-element.628) | copy-start | bytes 388 | tf_op jit(solution)/shard_map/while
  119.4 12.5 %copy-start.8 = (f32[64,1]{0,1:T(1,128)S(1)}, f32[64,1]{0,1:T(1,128)}, u32[]{:S(2)}) copy-start(f32[64,1]{0,1:T(1,128)} %get-tuple-element.626) | copy-start | bytes 772 | tf_op jit(solution)/shard_map/while
  122.8 9.3 %copy-start.15 = (f32[1,32]{1,0:T(1,128)S(1)}, f32[1,32]{1,0:T(1,128)}, u32[]{:S(2)}) copy-start(f32[1,32]{1,0:T(1,128)} %get-tuple-element.628) | copy-start | bytes 388 | tf_op jit(solution)/shard_map/while
  132.8 12.5 %copy-start.8 = (f32[64,1]{0,1:T(1,128)S(1)}, f32[64,1]{0,1:T(1,128)}, u32[]{:S(2)}) copy-start(f32[64,1]{0,1:T(1,128)} %get-tuple-element.626) | copy-start | bytes 772 | tf_op jit(solution)/shard_map/while
  136.2 9.3 %copy-start.15 = (f32[1,32]{1,0:T(1,128)S(1)}, f32[1,32]{1,0:T(1,128)}, u32[]{:S(2)}) copy-start(f32[1,32]{1,0:T(1,128)} %get-tuple-element.628) | copy-start | bytes 388 | tf_op jit(solution)/shard_map/while
  146.2 12.5 %copy-start.8 = (f32[64,1]{0,1:T(1,128)S(1)}, f32[64,1]{0,1:T(1,128)}, u32[]{:S(2)}) copy-start(f32[64,1]{0,1:T(1,128)} %get-tuple-element.626) | copy-start | bytes 772 | tf_op jit(solution)/shard_map/while
  149.7 9.3 %copy-start.15 = (f32[1,32]{1,0:T(1,128)S(1)}, f32[1,32]{1,0:T(1,128)}, u32[]{:S(2)}) copy-start(f32[1,32]{1,0:T(1,128)} %get-tuple-element.628) | copy-start | bytes 388 | tf_op jit(solution)/shard_map/while
  159.6 12.5 %copy-start.8 = (f32[64,1]{0,1:T(1,128)S(1)}, f32[64,1]{0,1:T(1,128)}, u32[]{:S(2)}) copy-start(f32[64,1]{0,1:T(1,128)} %get-tuple-element.626) | copy-start | bytes 772 | tf_op jit(solution)/shard_map/while
  173.0 12.5 %copy-start.8 = (f32[64,1]{0,1:T(1,128)S(1)}, f32[64,1]{0,1:T(1,128)}, u32[]{:S(2)}) copy-start(f32[64,1]{0,1:T(1,128)} %get-tuple-element.626) | copy-start | bytes 772 | tf_op jit(solution)/shard_map/while
  186.4 12.5 %copy-start.8 = (f32[64,1]{0,1:T(1,128)S(1)}, f32[64,1]{0,1:T(1,128)}, u32[]{:S(2)}) copy-start(f32[64,1]{0,1:T(1,128)} %get-tuple-element.626) | copy-start | bytes 772 | tf_op jit(solution)/shard_map/while
  189.9 9.3 %copy-start.15 = (f32[1,32]{1,0:T(1,128)S(1)}, f32[1,32]{1,0:T(1,128)}, u32[]{:S(2)}) copy-start(f32[1,32]{1,0:T(1,128)} %get-tuple-element.628) | copy-start | bytes 388 | tf_op jit(solution)/shard_map/while
  199.9 12.5 %copy-start.8 = (f32[64,1]{0,1:T(1,128)S(1)}, f32[64,1]{0,1:T(1,128)}, u32[]{:S(2)}) copy-start(f32[64,1]{0,1:T(1,128)} %get-tuple-element.626) | copy-start | bytes 772 | tf_op jit(solution)/shard_map/while
  213.3 12.5 %copy-start.8 = (f32[64,1]{0,1:T(1,128)S(1)}, f32[64,1]{0,1:T(1,128)}, u32[]{:S(2)}) copy-start(f32[64,1]{0,1:T(1,128)} %get-tuple-element.626) | copy-start | bytes 772 | tf_op jit(solution)/shard_map/while
  226.7 12.5 %copy-start.8 = (f32[64,1]{0,1:T(1,128)S(1)}, f32[64,1]{0,1:T(1,128)}, u32[]{:S(2)}) copy-start(f32[64,1]{0,1:T(1,128)} %get-tuple-element.626) | copy-start | bytes 772 | tf_op jit(solution)/shard_map/while
  240.1 12.5 %copy-start.8 = (f32[64,1]{0,1:T(1,128)S(1)}, f32[64,1]{0,1:T(1,128)}, u32[]{:S(2)}) copy-start(f32[64,1]{0,1:T(1,128)} %get-tuple-element.626) | copy-start | bytes 772 | tf_op jit(solution)/shard_map/while
  253.5 12.5 %copy-start.8 = (f32[64,1]{0,1:T(1,128)S(1)}, f32[64,1]{0,1:T(1,128)}, u32[]{:S(2)}) copy-start(f32[64,1]{0,1:T(1,128)} %get-tuple-element.626) | copy-start | bytes 772 | tf_op jit(solution)/shard_map/while
  266.9 12.5 %copy-start.8 = (f32[64,1]{0,1:T(1,128)S(1)}, f32[64,1]{0,1:T(1,128)}, u32[]{:S(2)}) copy-start(f32[64,1]{0,1:T(1,128)} %get-tuple-element.626) | copy-start | bytes 772 | tf_op jit(solution)/shard_map/while
  280.3 12.5 %copy-start.8 = (f32[64,1]{0,1:T(1,128)S(1)}, f32[64,1]{0,1:T(1,128)}, u32[]{:S(2)}) copy-start(f32[64,1]{0,1:T(1,128)} %get-tuple-element.626) | copy-start | bytes 772 | tf_op jit(solution)/shard_map/while
  283.8 9.3 %copy-start.15 = (f32[1,32]{1,0:T(1,128)S(1)}, f32[1,32]{1,0:T(1,128)}, u32[]{:S(2)}) copy-start(f32[1,32]{1,0:T(1,128)} %get-tuple-element.628) | copy-start | bytes 388 | tf_op jit(solution)/shard_map/while
  293.8 12.5 %copy-start.8 = (f32[64,1]{0,1:T(1,128)S(1)}, f32[64,1]{0,1:T(1,128)}, u32[]{:S(2)}) copy-start(f32[64,1]{0,1:T(1,128)} %get-tuple-element.626) | copy-start | bytes 772 | tf_op jit(solution)/shard_map/while
  321.9 115.4 %collective-permute-start.4 = (f32[2,5120,128]{1,2,0:T(8,128)S(1)}, f32[2,5120,128]{1,2,0:T(8,128)S(1)}, u32[]{:S(2)}, u32[]{:S(2)}) collective-permute-start(f32[2,5120,128]{1,2,0:T(8,128)S(1)} %pad_maximum_fusion), channel_id=1, source_target_pairs={{0,4},{4,0},{8,12},{12,8},{16,20},{20,16},{24,28},{28,24},{1,5},{5... | collective-permute-start | bytes 15728648 | tf_op jit(solution)/shard_map/ppermute | solution.py:174
  438.1 122.9 %copy-start.9 = (s32[4,8]{1,0:T(4,128)S(1)}, s32[4,8]{1,0:T(4,128)}, u32[]{:S(2)}) copy-start(s32[4,8]{1,0:T(4,128)} %param.46) | copy-start | bytes 388
  438.1 123.0 %copy-start.16 = (u32[32]{0:T(128)S(1)}, u32[32]{0:T(128)}, u32[]{:S(2)}) copy-start(u32[32]{0:T(128)} %constant.155) | copy-start | bytes 388
  438.1 114.6 %collective-permute-start.5 = (f32[2,5120,128]{1,2,0:T(8,128)S(1)}, f32[2,5120,128]{1,2,0:T(8,128)}, u32[]{:S(2)}, u32[]{:S(2)}) collective-permute-start(f32[2,5120,128]{1,2,0:T(8,128)S(1)} %fusion.80), channel_id=1, source_target_pairs={{0,8},{4,12},{8,0},{12,4},{16,24},{20,28},{24,16},{28,20},{1,9},{5... | collective-permute-start | bytes 15728648 | tf_op jit(solution)/shard_map/ppermute | solution.py:174
  558.8 227.2 %collective-permute-start.6 = (f32[2,5120,128]{1,2,0:T(8,128)}, f32[2,5120,128]{1,2,0:T(8,128)}, u32[]{:S(2)}, u32[]{:S(2)}) collective-permute-start(f32[2,5120,128]{1,2,0:T(8,128)} %fusion.85), channel_id=1, source_target_pairs={{0,16},{4,20},{8,24},{12,28},{16,0},{20,4},{24,8},{28,12},{1,17},{... | collective-permute-start | bytes 15728648 | tf_op jit(solution)/shard_map/ppermute | solution.py:174
  (14 other events, 114.9 us)
